TPU v7x, 512 devices: a whole 4x4x16 slice. The times are simulated.
512 devices in a mesh: seq: 32 (over x, y, core), heads: 4 (over z_lo), dp: 4 (over z_hi).
Axes of the slice: x: 4, y: 4, z: 16 (z_hi: 4, z_lo: 4; z = z_hi * 4 + z_lo), core: 2. Of those that a mesh axis runs over, the one named last changes fastest.
Arguments:
- activations: bfloat16 [16384, 8192], P(('dp', 'seq'), 'heads'), parts along dimension 0, may hold values from -6 to 6
- conv_taps: bfloat16 [4, 8192], P(None, 'heads'), may hold values from -3 to 3
- gate_in: bfloat16 [8192, 1024], P('heads', 'seq'), may hold values from -0.0625 to 0.0625
- gate_out: bfloat16 [1024, 8], replicated, may hold values from -0.59765625 to 0.59765625
- queries: bfloat16 [16384, 8192], P(('dp', 'seq'), 'heads'), parts along dimension 0, may hold values from -1000 to 1000, as said below
- key_vectors: bfloat16 [16384, 1024], P(('dp', 'seq'), 'heads'), parts along dimension 0, may hold values from -4 to 4, as said below
- value_vectors: bfloat16 [16384, 1024], P(('dp', 'seq'), 'heads'), parts along dimension 0, may hold values from -6 to 6
- segment_ids: int32 [16384], P('dp'), parts along dimension 0, may hold values from 0 to 3, never falling along the last dimension, each value on 1 to 2048 neighbouring positions
Outputs:
- attended: bfloat16 [16384, 8192], P(('dp', 'seq'), 'heads'), parts along dimension 0
- key_mass: bfloat16 [8, 16384], P('heads', ('dp', 'seq')), parts along dimension 1
There are 4 independent parts, one for each index of `dp`. A program takes and returns all parts, laid end to end along the dimension named above; an argument that names none is the same for every part. Nothing has to cross between parts.
Inputs may be any that keep to these rules, and one draw needn't show every extreme that they name: `queries`: finite. `key_vectors`: finite.
All inputs are finite; a program needn't handle non-finite values.
Results may differ from a plain program's by a relative error of at most 0.0056.
Values may be sent and summed in bfloat16 or wider, within the bound.
A program may use at most 64 MiB of HBM per device.

v0:
```python
import math

import jax
import jax.numpy as jnp
from jax import lax
from jax.sharding import PartitionSpec as P

QUERY_HEADS = 64
KV_HEADS = 8
HEAD_DIM = 128


NEG_FILL = -1e30


def from_behind(block, axis, distance):
    devices = range(lax.axis_size(axis))
    route = [(i - distance, i) for i in devices if i - distance in devices]
    return lax.ppermute(block, axis, route)


def partner(x, axis, distance):
    return lax.ppermute(x, axis, [(i, i ^ 1 << distance) for i in range(lax.axis_size(axis))])


def key_places(flat_index, shard_rows, seq_count):
    half_rows = shard_rows // 2
    owner_dev = flat_index // shard_rows
    within = flat_index % shard_rows
    block_index = jnp.where(within < half_rows, 2 * owner_dev, 2 * seq_count - 1 - 2 * owner_dev)
    return block_index * half_rows + within % half_rows


def block_scores(query_heads, key_block, bias_block, allowed, score_scale):
    scores = (
        jnp.einsum("tgeh,kgh->getk", query_heads, key_block, preferred_element_type=jnp.float32)
        * score_scale
    )
    scores = scores + jnp.transpose(bias_block.astype(jnp.float32))[:, None, None, :]
    return jnp.where(allowed[None, None], scores, NEG_FILL)


def per_device(
    activations, conv_taps, gate_in, gate_out, queries, key_vectors, value_vectors, segment_ids
):
    shard_rows = activations.shape[0]
    tap_count = conv_taps.shape[0]
    rim_rows = from_behind(activations[shard_rows - (tap_count - 1) :], "seq", 1)
    widened = jnp.concatenate([rim_rows, activations], 0).astype(jnp.float32)
    summed = jnp.zeros(activations.shape, jnp.float32)
    for shift_back in range(tap_count):
        start_row = tap_count - 1 - shift_back
        summed = (
            summed
            + conv_taps[shift_back].astype(jnp.float32)
            * widened[start_row : start_row + shard_rows]
        )
    mixed_rows = summed.astype(jnp.bfloat16)
    partial_hidden = jnp.dot(
        mixed_rows,
        lax.all_gather(gate_in, "seq", axis=1, tiled=True),
        preferred_element_type=jnp.float32,
    )
    kv_local = key_vectors.shape[1] // HEAD_DIM
    group_size = QUERY_HEADS // KV_HEADS
    head_rank = lax.axis_index("heads")
    hidden = jax.nn.silu(lax.psum(partial_hidden, "heads")).astype(jnp.bfloat16)
    logits = jnp.dot(hidden, gate_out, preferred_element_type=jnp.float32)
    retention = lax.dynamic_slice_in_dim(
        jax.nn.log_sigmoid(logits).astype(jnp.bfloat16), head_rank * kv_local, kv_local, 1
    )
    seq_count = lax.axis_size("seq")
    seq_rank = lax.axis_index("seq")
    half_rows = shard_rows // 2
    local_index = jnp.arange(shard_rows, dtype=jnp.int32)
    moved_half = (
        queries[half_rows:],
        key_vectors[half_rows:],
        value_vectors[half_rows:],
        retention[half_rows:],
    )
    for bit_number in range(seq_count.bit_length() - 1):
        moved_half = partner(
            (moved_half[0], moved_half[1], moved_half[2], moved_half[3]), "seq", bit_number
        )
    own_queries = jnp.concatenate([queries[:half_rows], moved_half[0]], 0)
    own_keys = jnp.concatenate([key_vectors[:half_rows], moved_half[1]], 0)
    own_values = jnp.concatenate([value_vectors[:half_rows], moved_half[2]], 0)
    own_bias = jnp.concatenate([retention[:half_rows], moved_half[3]], 0)
    query_places = jnp.where(
        local_index < half_rows,
        2 * seq_rank * half_rows + local_index,
        (2 * seq_count - 1 - 2 * seq_rank) * half_rows + local_index - half_rows,
    )
    query_segments = jnp.take(segment_ids, query_places)
    query_heads = own_queries.reshape(shard_rows, kv_local, group_size, HEAD_DIM)
    score_scale = 1.0 / math.sqrt(HEAD_DIM)

    def visibility(flat_index):
        places = key_places(flat_index, shard_rows, seq_count)
        key_segments = jnp.take(segment_ids, places)
        return (places[None, :] <= query_places[:, None]) & (
            key_segments[None, :] == query_segments[:, None]
        )

    initial = (
        jnp.full((kv_local, group_size, shard_rows), NEG_FILL, jnp.float32),
        jnp.zeros((kv_local, group_size, shard_rows), jnp.float32),
    )
    all_keys, all_values, all_bias = (
        lax.all_gather(own_keys, "seq", axis=0, tiled=True),
        lax.all_gather(own_values, "seq", axis=0, tiled=True),
        lax.all_gather(own_bias, "seq", axis=0, tiled=True),
    )
    piece_rows = all_keys.shape[0]
    stats_block_width = math.gcd(piece_rows, 512)

    def one_block(block_number, state_in):
        offset = block_number * stats_block_width
        key_block = lax.dynamic_slice_in_dim(all_keys, offset, stats_block_width, 0).reshape(
            stats_block_width, kv_local, HEAD_DIM
        )
        bias_block = lax.dynamic_slice_in_dim(all_bias, offset, stats_block_width, 0)
        allowed = visibility(0 + offset + jnp.arange(stats_block_width, dtype=jnp.int32))

        def update(state_old):
            peak_old, mass_old = state_old
            masked = block_scores(query_heads, key_block, bias_block, allowed, score_scale)
            peak_new = jnp.maximum(peak_old, jnp.max(masked, axis=3))
            exponent = jnp.where(allowed[None, None], jnp.exp(masked - peak_new[..., None]), 0.0)
            return (peak_new, mass_old * jnp.exp(peak_old - peak_new) + jnp.sum(exponent, axis=3))

        def keep_state(state_old):
            return state_old

        return lax.cond(jnp.any(allowed), update, keep_state, state_in)

    row_peak, total_mass = lax.fori_loop(0, piece_rows // stats_block_width, one_block, initial)
    total_keys = all_keys.shape[0]
    block_width = math.gcd(total_keys, 512)
    block_count = total_keys // block_width
    key_blocks = all_keys.reshape(block_count, block_width, kv_local, HEAD_DIM)
    value_blocks = all_values.reshape(block_count, block_width, kv_local, HEAD_DIM)
    bias_blocks = all_bias.reshape(block_count, block_width, kv_local)

    def second_pass(accumulated, block_items):
        block_number, key_block, value_block, bias_block = block_items
        allowed = visibility(block_number * block_width + jnp.arange(block_width, dtype=jnp.int32))

        def attend(accum_in):
            masked = block_scores(query_heads, key_block, bias_block, allowed, score_scale)
            weights = (
                jnp.where(allowed[None, None], jnp.exp(masked - row_peak[..., None]), 0.0)
                / total_mass[..., None]
            )
            accum_out = accum_in + jnp.einsum(
                "getk,kgh->tgeh",
                weights.astype(jnp.bfloat16),
                value_block,
                preferred_element_type=jnp.float32,
            )
            return (accum_out, jnp.transpose(jnp.sum(weights, axis=(1, 2))) / group_size)

        def skip_block(accum_in):
            return (accum_in, jnp.zeros((block_width, kv_local), jnp.float32))

        return lax.cond(jnp.any(allowed), attend, skip_block, accumulated)

    accumulated, mass_blocks = lax.scan(
        second_pass,
        jnp.zeros((shard_rows, kv_local, group_size, HEAD_DIM), jnp.float32),
        (jnp.arange(block_count, dtype=jnp.int32), key_blocks, value_blocks, bias_blocks),
    )
    key_term = mass_blocks.reshape(total_keys, kv_local)
    key_mass = lax.psum_scatter(key_term, "seq", scatter_dimension=0, tiled=True).astype(
        jnp.bfloat16
    )
    attended = accumulated.reshape(shard_rows, kv_local * group_size * HEAD_DIM).astype(
        jnp.bfloat16
    )
    returned = (attended[half_rows:], key_mass[half_rows:])
    for bit_number in range(seq_count.bit_length() - 1):
        returned = partner((returned[0], returned[1]), "seq", bit_number)
    attended = jnp.concatenate([attended[:half_rows], returned[0]], 0)
    key_mass = jnp.concatenate([key_mass[:half_rows], returned[1]], 0)
    return (attended, jnp.transpose(key_mass))


def solution(mesh):
    return jax.shard_map(
        per_device,
        mesh=mesh,
        in_specs=(
            P(("dp", "seq"), "heads"),
            P(None, "heads"),
            P("heads", "seq"),
            P(),
            P(("dp", "seq"), "heads"),
            P(("dp", "seq"), "heads"),
            P(("dp", "seq"), "heads"),
            P("dp"),
        ),
        out_specs=(P(("dp", "seq"), "heads"), P("heads", ("dp", "seq"))),
        check_vma=False,
    )
```

profile of v0, /device:TPU:1, one launch (start us, length us, event | category | flops | bytes accessed | tf_op | source)
XLA Modules:
  0.0 620.0 jit_solution(121066509790797617)
XLA Ops:
  8.7 4.6 collective-permute-start.10
  18.7 59.5 %all-gather.6.cloned.1.call-done = bf16[2048,1024]{0,1:T(8,128)(2,1)} async-done(((bf16[2048,32]{0,1:T(8,128)(2,1)}), bf16[2048,1024]{0,1:T(8,128)(2,1)}) %all-gather.6.cloned.1.call-update) | async-done | bytes 4194320 | tf_op jit(solution)/shard_map/all_gather | solution.py:61
  78.2 4.7 fusion.39
  91.2 4.1 collective-permute-start.2
  103.1 3.7 collective-permute-start.4
  110.5 6.4 %collective-permute-start.16 = (bf16[64,256]{1,0:T(8,128)(2,1)S(1)}, bf16[64,256]{1,0:T(8,128)(2,1)S(1)}, u32[]{:S(2)}, u32[]{:S(2)}) collective-permute-start(bf16[64,256]{1,0:T(8,128)(2,1)S(1)} %get-tuple-element.851), channel_id=1, source_target_pairs={{0,16},{16,0},{32,48},{48,32},{64,80},{80,64},{96,112},{112,96},{1... | collective-permute-start | bytes 98312 | tf_op jit(solution)/shard_map/ppermute | solution.py:23
  122.3 3.7 collective-permute-start.18
  133.1 3.8 collective-permute-start.20
  140.7 6.5 %collective-permute-start.5 = (bf16[64,2048]{0,1:T(8,128)(2,1)S(1)}, bf16[64,2048]{0,1:T(8,128)(2,1)S(1)}, u32[]{:S(2)}, u32[]{:S(2)}) collective-permute-start(bf16[64,2048]{0,1:T(8,128)(2,1)S(1)} %copy.51), channel_id=1, source_target_pairs={{0,16},{16,0},{32,48},{48,32},{64,80},{80,64},{96,112},{112,96},{1... | collective-permute-start | bytes 786440 | tf_op jit(solution)/shard_map/ppermute | solution.py:23
  151.5 12.2 %collective-permute-done.6 = bf16[64,2048]{0,1:T(8,128)(2,1)S(1)} collective-permute-done((bf16[64,2048]{0,1:T(8,128)(2,1)S(1)}, bf16[64,2048]{0,1:T(8,128)(2,1)S(1)}, u32[]{:S(2)}, u32[]{:S(2)}) %collective-permute-start.6) | collective-permute-done | bytes 262176 | tf_op jit(solution)/shard_map/ppermute | solution.py:23
  163.7 3.8 collective-permute-start.7
  167.5 12.6 %collective-permute-done.7 = bf16[64,2048]{0,1:T(8,128)(2,1)S(1)} collective-permute-done((bf16[64,2048]{0,1:T(8,128)(2,1)S(1)}, bf16[64,2048]{0,1:T(8,128)(2,1)S(1)}, u32[]{:S(2)}, u32[]{:S(2)}) %collective-permute-start.7) | collective-permute-done | bytes 262176 | tf_op jit(solution)/shard_map/ppermute | solution.py:23
  182.9 10.5 %collective-permute-done.8 = bf16[64,2048]{0,1:T(8,128)(2,1)S(1)} collective-permute-done((bf16[64,2048]{0,1:T(8,128)(2,1)S(1)}, bf16[64,2048]{0,1:T(8,128)(2,1)S(1)}, u32[]{:S(2)}, u32[]{:S(2)}) %collective-permute-start.8) | collective-permute-done | bytes 262176 | tf_op jit(solution)/shard_map/ppermute | solution.py:23
  193.3 4.3 collective-permute-start.9
  199.1 4.9 collective-permute-start.11
  221.0 3.7 collective-permute-start.15
  227.7 51.3 %all-gather.8.cloned.1.call-done = bf16[4096,256]{1,0:T(8,128)(2,1)} async-done(((bf16[128,256]{1,0:T(8,128)(2,1)}), bf16[4096,256]{1,0:T(8,128)(2,1)}) %all-gather.8.cloned.1.call-update) | async-done | bytes 2097168 | tf_op jit(solution)/shard_map/all_gather | solution.py:112
  283.4 20.8 %all_gather.14 = bf16[4096,2]{0,1:T(2,128)(2,1)S(1)} all-gather(bf16[128,2]{0,1:T(2,128)(2,1)S(1)} %pad_maximum_fusion.4), channel_id=1, replica_groups=mesh['seq'=32,'heads'=4,'dp'=4] {'seq'}, dimensions={0}, use_global_device_ids=true | all-gather | bytes 16896 | tf_op jit(solution)/shard_map/all_gather | solution.py:113
  304.2 63.0 %while.38 = (s32[]{:T(128)}, f32[2,8,128]{2,1,0:T(8,128)S(1)}, f32[2,8,128]{2,1,0:T(8,128)S(1)}, s32[4096]{0:T(1024)S(1)}, s32[128]{0:T(128)S(1)}, /*index=5*/bf...) while((s32[]{:T(128)}, f32[2,8,128]{2,1,0:T(8,128)S(1)}, ...), condition=%wide.region_7.9_spmd.clone, body=%wide.region_1.8_spmd.clone.sunk | while | flops 279233152 | bytes 10043169 | solution.py:138
  367.3 79.6 %while.39 = (s32[]{:T(128)}, f32[128,2,8,128]{3,0,2,1:T(8,128)S(1)}, f32[8,512,2]{1,2,0:T(2,128)S(1)}, s32[8]{0:T(128)S(1)}, s32[4096]{0:T(1024)S(1)}, /*index=5...) while((s32[]{:T(128)}, ...), condition=%wide.region_13.15_spmd.clone, body=%wide.region_8.14_spmd.clone.sunk | while | flops 545829504 | bytes 7545635 | solution.py:169
  373.2 4.6 conditional.7
  383.7 4.6 conditional.7
  394.2 4.6 conditional.7
  404.7 4.6 conditional.7
  421.2 4.6 conditional.7
  431.7 4.6 conditional.7
  442.2 4.6 conditional.7
  453.2 7.1 %collective-permute-done.22 = bf16[64,2048]{1,0:T(8,128)(2,1)S(1)} collective-permute-done((bf16[64,2048]{1,0:T(8,128)(2,1)S(1)}, bf16[64,2048]{1,0:T(8,128)(2,1)S(1)}, u32[]{:S(2)}, u32[]{:S(2)}) %collective-permute-start.22) | collective-permute-done | bytes 262176 | tf_op jit(solution)/shard_map/ppermute | solution.py:23
  462.2 8.3 %collective-permute-done.23 = bf16[64,2048]{1,0:T(8,128)(2,1)S(1)} collective-permute-done((bf16[64,2048]{1,0:T(8,128)(2,1)S(1)}, bf16[64,2048]{1,0:T(8,128)(2,1)S(1)}, u32[]{:S(2)}, u32[]{:S(2)}) %collective-permute-start.23) | collective-permute-done | bytes 262176 | tf_op jit(solution)/shard_map/ppermute | solution.py:23
  474.5 106.6 %reduce-scatter.4.cloned.1.call-done = f32[128,2]{1,0:T(8,128)} async-done(((f32[4096,2]{1,0:T(8,128)}), f32[128,2]{1,0:T(8,128)}) %reduce-scatter.4.cloned.1.call-update) | async-done | bytes 1040
  582.1 3.7 collective-permute-start.25
  585.8 5.1 collective-permute-start.26
  (307 shorter events, 260.3 us)
Async XLA Ops:
  7.2 71.0 %all-gather.6.cloned.1.call-start = ((), (), s32[]{:S(2)}) async-start(), calls=%async_computation.2 | async-start | bytes 4325376 | tf_op jit(solution)/shard_map/all_gather | solution.py:61
  7.9 189.7 %all-reduce.2.cloned.1.call-start = ((), (), s32[]{:S(2)}) async-start(), calls=%async_computation.3 | async-start | bytes 1048576 | tf_op jit(solution)/shard_map/psum | solution.py:67
  8.7 8.8 %collective-permute-start.10 = (bf16[3,2048]{1,0:T(4,128)(2,1)S(1)}, bf16[3,2048]{1,0:T(4,128)(2,1)S(1)}, u32[]{:S(2)}, u32[]{:S(2)}) collective-permute-start(bf16[3,2048]{1,0:T(4,128)(2,1)S(1)} %slice.74), channel_id=1, source_target_pairs={{0,16},{16,32},{32,48},{48,64},{64,80},{80,96},{96,112},{112,128},... | collective-permute-start | bytes 36872 | tf_op jit(solution)/shard_map/ppermute | solution.py:19
  82.9 135.6 %all-gather.4.cloned.1.call-start = ((), (), s32[]{:S(2)}) async-start(), calls=%async_computation.1 | async-start | bytes 2162688 | tf_op jit(solution)/shard_map/all_gather | solution.py:111
  86.2 5.0 collective-permute-start.1
  91.2 6.5 %collective-permute-start.2 = (bf16[64,256]{0,1:T(8,128)(2,1)S(1)}, bf16[64,256]{0,1:T(8,128)(2,1)S(1)}, u32[]{:S(2)}, u32[]{:S(2)}) collective-permute-start(bf16[64,256]{0,1:T(8,128)(2,1)S(1)} %collective-permute-done.1), channel_id=1, source_target_pairs={{0,64},{16,80},{32,96},{48,112},{64,0},{80,16},{96,32},{112,48},{1... | collective-permute-start | bytes 98312 | tf_op jit(solution)/shard_map/ppermute | solution.py:23
  97.7 5.4 collective-permute-start.3
  103.1 6.5 %collective-permute-start.4 = (bf16[64,256]{0,1:T(8,128)(2,1)S(1)}, bf16[64,256]{0,1:T(8,128)(2,1)S(1)}, u32[]{:S(2)}, u32[]{:S(2)}) collective-permute-start(bf16[64,256]{0,1:T(8,128)(2,1)S(1)} %collective-permute-done.3), channel_id=1, source_target_pairs={{0,256},{16,272},{32,288},{48,304},{64,320},{80,336},{96,352},{112... | collective-permute-start | bytes 98312 | tf_op jit(solution)/shard_map/ppermute | solution.py:23
  110.4 168.6 %all-gather.8.cloned.1.call-start = ((), (), s32[]{:S(2)}) async-start(), calls=%async_computation.4 | async-start | bytes 2162688 | tf_op jit(solution)/shard_map/all_gather | solution.py:112
  110.5 7.2 %collective-permute-start.16 = (bf16[64,256]{1,0:T(8,128)(2,1)S(1)}, bf16[64,256]{1,0:T(8,128)(2,1)S(1)}, u32[]{:S(2)}, u32[]{:S(2)}) collective-permute-start(bf16[64,256]{1,0:T(8,128)(2,1)S(1)} %get-tuple-element.851), channel_id=1, source_target_pairs={{0,16},{16,0},{32,48},{48,32},{64,80},{80,64},{96,112},{112,96},{1... | collective-permute-start | bytes 98312 | tf_op jit(solution)/shard_map/ppermute | solution.py:23
  117.7 4.6 collective-permute-start.17
  122.3 6.2 collective-permute-start.18
  128.5 4.6 collective-permute-start.19
  133.1 6.5 %collective-permute-start.20 = (bf16[64,256]{1,0:T(8,128)(2,1)S(1)}, bf16[64,256]{1,0:T(8,128)(2,1)S(1)}, u32[]{:S(2)}, u32[]{:S(2)}) collective-permute-start(bf16[64,256]{1,0:T(8,128)(2,1)S(1)} %collective-permute-done.19), channel_id=1, source_target_pairs={{0,256},{16,272},{32,288},{48,304},{64,320},{80,336},{96,352},{112... | collective-permute-start | bytes 98312 | tf_op jit(solution)/shard_map/ppermute | solution.py:23
  140.3 440.9 %reduce-scatter.4.cloned.1.call-start = ((), (), s32[]{:S(2)}) async-start(), calls=%async_computation.5 | async-start | bytes 2162688
  140.7 8.0 %collective-permute-start.5 = (bf16[64,2048]{0,1:T(8,128)(2,1)S(1)}, bf16[64,2048]{0,1:T(8,128)(2,1)S(1)}, u32[]{:S(2)}, u32[]{:S(2)}) collective-permute-start(bf16[64,2048]{0,1:T(8,128)(2,1)S(1)} %copy.51), channel_id=1, source_target_pairs={{0,16},{16,0},{32,48},{48,32},{64,80},{80,64},{96,112},{112,96},{1... | collective-permute-start | bytes 786440 | tf_op jit(solution)/shard_map/ppermute | solution.py:23
  148.7 15.0 %collective-permute-start.6 = (bf16[64,2048]{0,1:T(8,128)(2,1)S(1)}, bf16[64,2048]{0,1:T(8,128)(2,1)S(1)}, u32[]{:S(2)}, u32[]{:S(2)}) collective-permute-start(bf16[64,2048]{0,1:T(8,128)(2,1)S(1)} %collective-permute-done.5), channel_id=1, source_target_pairs={{0,32},{16,48},{32,0},{48,16},{64,96},{80,112},{96,64},{112,80},{1... | collective-permute-start | bytes 786440 | tf_op jit(solution)/shard_map/ppermute | solution.py:23
  163.7 16.3 %collective-permute-start.7 = (bf16[64,2048]{0,1:T(8,128)(2,1)S(1)}, bf16[64,2048]{0,1:T(8,128)(2,1)S(1)}, u32[]{:S(2)}, u32[]{:S(2)}) collective-permute-start(bf16[64,2048]{0,1:T(8,128)(2,1)S(1)} %collective-permute-done.6), channel_id=1, source_target_pairs={{0,64},{16,80},{32,96},{48,112},{64,0},{80,16},{96,32},{112,48},{1... | collective-permute-start | bytes 786440 | tf_op jit(solution)/shard_map/ppermute | solution.py:23
  180.0 13.3 %collective-permute-start.8 = (bf16[64,2048]{0,1:T(8,128)(2,1)S(1)}, bf16[64,2048]{0,1:T(8,128)(2,1)S(1)}, u32[]{:S(2)}, u32[]{:S(2)}) collective-permute-start(bf16[64,2048]{0,1:T(8,128)(2,1)S(1)} %collective-permute-done.7), channel_id=1, source_target_pairs={{0,128},{16,144},{32,160},{48,176},{64,192},{80,208},{96,224},{112... | collective-permute-start | bytes 786440 | tf_op jit(solution)/shard_map/ppermute | solution.py:23
  193.3 19.8 %collective-permute-start.9 = (bf16[64,2048]{0,1:T(8,128)(2,1)S(1)}, bf16[64,2048]{0,1:T(8,128)(2,1)S(1)}, u32[]{:S(2)}, u32[]{:S(2)}) collective-permute-start(bf16[64,2048]{0,1:T(8,128)(2,1)S(1)} %collective-permute-done.8), channel_id=1, source_target_pairs={{0,256},{16,272},{32,288},{48,304},{64,320},{80,336},{96,352},{112... | collective-permute-start | bytes 786440 | tf_op jit(solution)/shard_map/ppermute | solution.py:23
  199.1 6.1 collective-permute-start.11
  205.2 4.6 collective-permute-start.12
  209.8 5.8 collective-permute-start.13
  215.6 5.4 collective-permute-start.14
  221.0 62.3 %collective-permute-start.15 = (bf16[64,2]{0,1:T(2,128)(2,1)S(1)}, bf16[64,2]{0,1:T(2,128)(2,1)S(1)}, u32[]{:S(2)}, u32[]{:S(2)}) collective-permute-start(bf16[64,2]{0,1:T(2,128)(2,1)S(1)} %collective-permute-done.14), channel_id=1, source_target_pairs={{0,256},{16,272},{32,288},{48,304},{64,320},{80,336},{96,352},{112... | collective-permute-start | bytes 776 | tf_op jit(solution)/shard_map/ppermute | solution.py:23
  450.7 9.6 %collective-permute-start.22 = (bf16[64,2048]{1,0:T(8,128)(2,1)S(1)}, bf16[64,2048]{1,0:T(8,128)(2,1)S(1)}, u32[]{:S(2)}, u32[]{:S(2)}) collective-permute-start(bf16[64,2048]{1,0:T(8,128)(2,1)S(1)} %collective-permute-done.21), channel_id=1, source_target_pairs={{0,32},{16,48},{32,0},{48,16},{64,96},{80,112},{96,64},{112,80},{1... | collective-permute-start | bytes 786440 | tf_op jit(solution)/shard_map/ppermute | solution.py:23
  460.3 10.2 %collective-permute-start.23 = (bf16[64,2048]{1,0:T(8,128)(2,1)S(1)}, bf16[64,2048]{1,0:T(8,128)(2,1)S(1)}, u32[]{:S(2)}, u32[]{:S(2)}) collective-permute-start(bf16[64,2048]{1,0:T(8,128)(2,1)S(1)} %collective-permute-done.22), channel_id=1, source_target_pairs={{0,64},{16,80},{32,96},{48,112},{64,0},{80,16},{96,32},{112,48},{1... | collective-permute-start | bytes 786440 | tf_op jit(solution)/shard_map/ppermute | solution.py:23
  470.5 111.6 %collective-permute-start.24 = (bf16[64,2048]{1,0:T(8,128)(2,1)S(1)}, bf16[64,2048]{1,0:T(8,128)(2,1)S(1)}, u32[]{:S(2)}, u32[]{:S(2)}) collective-permute-start(bf16[64,2048]{1,0:T(8,128)(2,1)S(1)} %collective-permute-done.23), channel_id=1, source_target_pairs={{0,128},{16,144},{32,160},{48,176},{64,192},{80,208},{96,224},{112... | collective-permute-start | bytes 786440 | tf_op jit(solution)/shard_map/ppermute | solution.py:23
  582.1 30.5 %collective-permute-start.25 = (bf16[64,2048]{1,0:T(8,128)(2,1)S(1)}, bf16[64,2048]{1,0:T(8,128)(2,1)S(1)}, u32[]{:S(2)}, u32[]{:S(2)}) collective-permute-start(bf16[64,2048]{1,0:T(8,128)(2,1)S(1)} %collective-permute-done.24), channel_id=1, source_target_pairs={{0,256},{16,272},{32,288},{48,304},{64,320},{80,336},{96,352},{112... | collective-permute-start | bytes 786440 | tf_op jit(solution)/shard_map/ppermute | solution.py:23
  585.8 5.9 collective-permute-start.26
  596.1 5.8 collective-permute-start.28
  606.2 5.8 collective-permute-start.30
  (9 other events, 426.1 us)
Sparse Core Ops, SparseCore 0:
  11.1 67.0 all-gather.5
  83.0 59.4 all-reduce.1
  145.6 70.1 all-gather.3
  218.8 60.1 all-gather.7
  474.7 106.4 reduce-scatter.3
where the time goes:
time: 627 us; the launch traced here: 620 us
  waiting for transfers between devices  311 us (50%)
  starting transfers between devices  104 us (17%)
  local copies, waits for them, and re-layouts  78.5 us (13%)
  matrix products  46 us (7%)
  other arithmetic  28.3 us (5%)
  blocking collectives  20.8 us (3%)
  loops' own time  17.7 us (3%)
  between operations  14.3 us (2%)
    unnamed x6, waiting for transfers between devices  107 us
    ppermute x30, starting transfers between devices, partner(): lax.ppermute(x, axis, [(i, i ^ 1 << distance) for i in range(lax.axis_siz...  98.9 us
    ppermute x30, waiting for transfers between devices, partner(): lax.ppermute(x, axis, [(i, i ^ 1 << distance) for i in range(lax.axis_siz...  89.2 us
    all_gather x1, waiting for transfers between devices, per_device(): lax.all_gather(gate_in, 'seq', axis=1, tiled=True)  59.5 us
    all_gather x1, waiting for transfers between devices, per_device(): lax.all_gather(own_values, 'seq', axis=0, tiled=True)  51.3 us
    gather x16, local copies, waits for them, and re-layouts, visibility(): key_segments = jnp.take(segment_ids, places)  50.3 us
    dot_general x14, matrix products, block_scores(): jnp.einsum('tgeh,kgh->getk', query_heads, key_block, preferred_element_ty...  28 us
    all_gather x1, blocking collectives, per_device(): lax.all_gather(own_bias, 'seq', axis=0, tiled=True)  20.8 us
  transfers between devices with their start and end apart: 36, of which 28 were waited for; matrix products, arithmetic and copies ran while one was open for 4% of the time, Pallas kernels for 0%

commit v1 on v0

v1 whole, which is shorter than its diff:
```python
import math

import jax
import jax.numpy as jnp
from jax import lax
from jax.experimental import pallas as pl
from jax.experimental.pallas import tpu as pltpu
from jax.sharding import PartitionSpec as P

MESH = pl.DeviceIdType.MESH
HEAD_DIM = 128
NEG = -1e30
SIDE = 4
CHIPS = SIDE * SIDE
WINDOW = 8
NT = (((1,), (1,)), ((), ()))

GATHER = 20
SEM_SWAP = 4 * GATHER
SEM_HALO = SEM_SWAP + 4
SEM_Z = SEM_HALO + 2
SEM_LOGIT = SEM_Z + 12
SEM_RET = SEM_LOGIT + 8
SEM_MASS = SEM_RET + 16
SEM_OUT = SEM_MASS + 18
SEMS = SEM_OUT + 1


def kernel(
    act_ref, taps_ref, wt_ref, gout_ref, q_ref, k_ref, v_ref, seg_ref,
    att_ref, mass_ref,
    rows_buf, mixed, wg, part, zrecv, lrecv, rown, rall, kvg, qbuf, obuf, orecv, sbuf, rel,
    colacc, colout, krecv, send_sem, recv_sem, local_sem,
):
    seq = lax.axis_index("seq")
    h = lax.axis_index("heads")
    c = lax.rem(seq, 2)
    ch = seq // 2
    x = ch // SIDE
    y = lax.rem(ch, SIDE)
    other = 1 - c
    shard_rows = act_ref.shape[0]
    half_q = q_ref.shape[1] // 2

    def at_chip(chip, core):
        return {"seq": lax.rem(chip, CHIPS) * 2 + core}

    def at_xy(xx, yy):
        return {"seq": (lax.rem(xx, SIDE) * SIDE + lax.rem(yy, SIDE)) * 2 + c}

    partner = {"seq": ch * 2 + other}

    barrier = pltpu.get_barrier_semaphore()

    def greet(i, carry):
        pl.semaphore_signal(
            barrier, inc=1, device_id={"seq": lax.rem(seq + i, 2 * CHIPS)}, device_id_type=MESH
        )
        return carry

    lax.fori_loop(1, 2 * CHIPS, greet, 0)
    for j in range(1, 4):
        for core in range(2):
            pl.semaphore_signal(
                barrier, inc=1, device_id={"seq": ch * 2 + core, "heads": lax.rem(h + j, 4)},
                device_id_type=MESH,
            )
    pl.semaphore_wait(barrier, 2 * CHIPS - 1 + 6)

    pending = []

    def send(src, dst, sem, device, rsem=None):
        copy = pltpu.make_async_remote_copy(
            src_ref=src, dst_ref=dst, send_sem=send_sem.at[sem],
            recv_sem=recv_sem.at[sem if rsem is None else rsem],
            device_id=device, device_id_type=MESH,
        )
        copy.start()
        pending.append(copy)

    def recv(slot, sem):
        pltpu.make_async_remote_copy(
            src_ref=slot, dst_ref=slot, send_sem=send_sem.at[sem], recv_sem=recv_sem.at[sem],
            device_id=partner, device_id_type=MESH,
        ).wait_recv()

    def axis_one(t, step):
        return at_xy(x + step, y) if t == 0 else at_xy(x, y + step)

    def axis_two(t, step):
        return at_xy(x, y + step) if t == 0 else at_xy(x + step, y)

    def place(t, i):
        own = x if t == 0 else y
        return lax.rem(own + (0, 3, 1, 2)[i], SIDE)

    def wslot(t, d, i, ab=None):
        p = place(t, i)
        return wg.at[:, d, t, p] if ab is None else wg.at[ab, d, t, p]

    def kvslot(t, d, i, ab=None):
        p = place(t, i)
        return kvg.at[t, d, p] if ab is None else kvg.at[t, d, p, ab]

    def second_sends(slot, base, t, i, src=None):
        source = slot(t, 0, i) if src is None else src
        sem = base + t * GATHER + 4 + 4 * i
        send(source, slot(t, 3, i), sem, axis_two(t, 1))
        send(source, slot(t, 1, i), sem + 1, axis_two(t, 3))

    def gather_start(slot, base, source):
        for t in range(2):
            sem = base + t * GATHER
            send(source(t), slot(t, 0, 0), sem, axis_one(t, 1))
            send(source(t), slot(t, 0, 0), sem + 1, axis_one(t, 3))
        for t in range(2):
            second_sends(slot, base, t, 0, source(t))

    def gather_first(slot, base):
        for t in range(2):
            sem = base + t * GATHER
            recv(slot(t, 0, 1), sem)
            send(slot(t, 0, 1, 0), slot(t, 0, 1, 0), sem + 2, axis_one(t, 1))
            recv(slot(t, 0, 2), sem + 1)
            send(slot(t, 0, 2, 1), slot(t, 0, 2, 1), sem + 3, axis_one(t, 3))
        for i in (1, 2):
            for t in range(2):
                second_sends(slot, base, t, i)
        for t in range(2):
            sem = base + t * GATHER
            recv(slot(t, 0, 3, 0), sem + 2)
            recv(slot(t, 0, 3, 1), sem + 3)
            second_sends(slot, base, t, 3)

    def gather_second(slot, base):
        for i in range(4):
            for t in range(2):
                sem = base + t * GATHER + 4 + 4 * i
                recv(slot(t, 3, i), sem)
                send(slot(t, 3, i, 0), slot(t, 2, i, 0), sem + 2, axis_two(t, 1))
                recv(slot(t, 1, i), sem + 1)
                send(slot(t, 1, i, 1), slot(t, 2, i, 1), sem + 3, axis_two(t, 3))

    def gather_last(slot, base):
        for i in range(4):
            for t in range(2):
                sem = base + t * GATHER + 4 + 4 * i
                recv(slot(t, 2, i, 0), sem + 2)
                recv(slot(t, 2, i, 1), sem + 3)

    W_BASE, KV_BASE = 0, 2 * GATHER
    gather_start(wslot, W_BASE, lambda t: wt_ref.at[t])

    own_rows = pl.ds(pl.multiple_of(c * shard_rows, 128), shard_rows)
    own_rows_in = pl.ds(pl.multiple_of(c * shard_rows + 16, 16), shard_rows)
    send(act_ref, rows_buf.at[own_rows_in], SEM_SWAP, partner)

    @pl.when(c == 1)
    def _():
        for core in range(2):
            pltpu.make_async_remote_copy(
                src_ref=act_ref.at[shard_rows - 16 : shard_rows], dst_ref=rows_buf.at[0:16],
                send_sem=send_sem.at[SEM_HALO + core], recv_sem=recv_sem.at[SEM_HALO],
                device_id=at_chip(ch + 1, core), device_id_type=MESH,
            ).start()

    def columns(which, width):
        return pl.ds(pl.multiple_of(which * width, width), width)

    send(k_ref.at[:, columns(other, 128)], kvg.at[0, 0, x, c], SEM_SWAP + 2, partner)
    send(v_ref.at[:, columns(other, 128)], kvg.at[1, 0, y, c], SEM_SWAP + 3, partner)
    send(q_ref.at[:, columns(other, half_q)], qbuf.at[own_rows], SEM_SWAP + 1, partner)
    local = [
        pltpu.make_async_copy(act_ref, rows_buf.at[own_rows_in], local_sem.at[0]),
        pltpu.make_async_copy(wt_ref.at[0], wslot(0, 0, 0), local_sem.at[1]),
        pltpu.make_async_copy(wt_ref.at[1], wslot(1, 0, 0), local_sem.at[2]),
        pltpu.make_async_copy(k_ref.at[:, columns(c, 128)], kvg.at[0, 0, x, c], local_sem.at[3]),
        pltpu.make_async_copy(v_ref.at[:, columns(c, 128)], kvg.at[1, 0, y, c], local_sem.at[4]),
        pltpu.make_async_copy(q_ref.at[:, columns(c, half_q)], qbuf.at[own_rows], local_sem.at[5]),
    ]
    for copy in local:
        copy.start()

    gather_first(wslot, W_BASE)

    recv(rows_buf.at[0:16], SEM_HALO)
    recv(rows_buf.at[pl.ds(pl.multiple_of(other * shard_rows + 16, 16), shard_rows)], SEM_SWAP)
    for copy in local:
        copy.wait()

    @pl.when(ch == 0)
    def _():
        rows_buf[0:16, :] = jnp.zeros((16, rows_buf.shape[1]), jnp.bfloat16)

    width = 512
    tap_count = taps_ref.shape[0]

    def mix(step, carry):
        r0 = pl.multiple_of((step // 4) * 64, 64)
        cols = pl.ds(pl.multiple_of(lax.rem(step, 4) * width, width), width)
        block = rows_buf[pl.ds(r0, 80), cols].astype(jnp.float32)
        total = jnp.zeros((64, width), jnp.float32)
        for tap in range(tap_count):
            moved = block if tap == 0 else pltpu.roll(block, tap, axis=0)
            total = total + taps_ref[tap : tap + 1, cols].astype(jnp.float32) * moved[16:80]
        mixed[pl.ds(r0, 64), cols] = total.astype(jnp.bfloat16)
        return carry

    lax.fori_loop(0, (2 * shard_rows // 64) * (mixed.shape[1] // width), mix, 0)

    def gate_group(d):
        depth = mixed.shape[1] // 2
        total = None
        for ab in range(2):
            term = lax.dot_general(
                mixed[:, ab * depth : (ab + 1) * depth],
                wg[ab, d].reshape(128, depth), NT, preferred_element_type=jnp.float32,
            )
            total = term if total is None else total + term
        part[d] = total
        for j in range(1, 4):
            peer = lax.rem(h + j, 4)
            send(
                part.at[d, pl.ds(pl.multiple_of(peer * 64, 64), 64)], zrecv.at[d, j - 1],
                SEM_Z + 3 * d + j - 1, {"heads": peer},
            )

    gate_group(0)
    gather_second(wslot, W_BASE)

    recv(kvg.at[0, 0, x, other], SEM_SWAP + 2)
    recv(kvg.at[1, 0, y, other], SEM_SWAP + 3)
    gather_start(kvslot, KV_BASE, lambda t: kvslot(t, 0, 0))

    gate_group(3)
    gate_group(1)
    gather_last(wslot, W_BASE)
    gate_group(2)

    gather_first(kvslot, KV_BASE)

    logits = jnp.zeros((8, 64), jnp.float32)
    for d in (0, 3, 1, 2):
        for j in range(3):
            recv(zrecv.at[d, j], SEM_Z + 3 * d + j)
        pre = part[d, pl.ds(pl.multiple_of(h * 64, 64), 64), :]
        pre = pre + zrecv[d, 0] + zrecv[d, 1] + zrecv[d, 2]
        hidden = (pre / (1.0 + jnp.exp(-pre))).astype(jnp.bfloat16)
        gout = gout_ref[c, 0, lax.rem(y + d, SIDE)] + gout_ref[c, 1, lax.rem(x + d, SIDE)]
        logits = logits + lax.dot_general(gout, hidden, NT, preferred_element_type=jnp.float32)
    mine = 2 * h + c
    lrecv[mine] = jnp.concatenate([logits, jnp.zeros((8, 64), jnp.float32)], 1)
    for j in range(4):
        for flip in range(2):
            if j or flip:
                peer, core = lax.rem(h + j, 4), lax.rem(c + flip, 2)
                send(
                    lrecv.at[mine], lrecv.at[mine], SEM_LOGIT + 2 * j + flip,
                    {"seq": ch * 2 + core, "heads": peer},
                )

    gather_second(kvslot, KV_BASE)

    for j in range(4):
        for flip in range(2):
            if j or flip:
                peer, core = lax.rem(h + 4 - j, 4), lax.rem(c + flip, 2)
                recv(lrecv.at[2 * peer + core], SEM_LOGIT + 2 * j + flip)
    lane = lax.broadcasted_iota(jnp.int32, (8, 128), 1)
    for block in range(2):
        low = lrecv[4 * block] + lrecv[4 * block + 1]
        high = pltpu.roll(lrecv[4 * block + 2] + lrecv[4 * block + 3], 64, axis=1)
        value = jnp.where(lane < 64, low, high)
        sig = jnp.minimum(value, 0.0) - jnp.log1p(jnp.exp(-jnp.abs(value)))
        rown[block] = sig.astype(jnp.bfloat16).astype(jnp.float32)
    for block in range(2):
        rall[ch, block : block + 1, :] = rown[block, pl.ds(mine, 1), :]
    for i in range(1, CHIPS):
        send(rall.at[ch], rall.at[ch], SEM_RET + i, at_chip(ch + i, c))

    gather_last(kvslot, KV_BASE)
    recv(qbuf.at[pl.ds(pl.multiple_of(other * shard_rows, 128), shard_rows)], SEM_SWAP + 1)

    rows = 2 * shard_rows
    pos = (ch * rows + lax.broadcasted_iota(jnp.int32, (rows, rows), 0)).astype(jnp.float32)
    first = jnp.zeros((rows, rows), jnp.float32)
    seg = seg_ref[...]
    for number in range(1, 4):
        count = jnp.sum((seg < number).astype(jnp.float32), axis=1, keepdims=True)
        count = jnp.sum(count, axis=0, keepdims=True)
        first = jnp.where(pos >= count, jnp.maximum(first, count), first)
    rel[...] = first - lax.broadcasted_iota(jnp.int32, (rows, rows), 1).astype(jnp.float32)
    colacc[...] = jnp.zeros_like(colacc)

    for i in range(1, CHIPS):
        recv(rall.at[lax.rem(ch + CHIPS - i, CHIPS)], SEM_RET + i)

    scale = 1.0 / math.sqrt(HEAD_DIM)
    blocks = range(WINDOW + 1)

    def chip_of(b):
        return lax.rem(ch + CHIPS - WINDOW + b, CHIPS)

    def head(e, carry):
        cols = pl.ds(pl.multiple_of(e * HEAD_DIM, HEAD_DIM), HEAD_DIM)
        query = qbuf[:, cols]
        peak = jnp.full((rows, 128), NEG, jnp.float32)
        for b in blocks:
            chip = chip_of(b)
            kx, ky = chip // SIDE, lax.rem(chip, SIDE)
            keys = kvg[0, lax.rem(ky + SIDE - y, SIDE), kx].reshape(rows, HEAD_DIM)
            bias = rall[chip]
            scores = lax.dot_general(query, keys, NT, preferred_element_type=jnp.float32) * scale
            start = ((ch - WINDOW + b) * rows).astype(jnp.float32)
            for half in range(2):
                lanes = slice(128 * half, 128 * half + 128)
                piece = scores[:, lanes] + bias[half : half + 1]
                seen = rel[:, lanes] <= start
                if b == WINDOW:
                    seen = seen & (
                        lax.broadcasted_iota(jnp.int32, (rows, 128), 1) + 128 * half
                        <= lax.broadcasted_iota(jnp.int32, (rows, 128), 0)
                    )
                piece = jnp.where(seen, piece, NEG)
                sbuf[b, :, lanes] = piece
                peak = jnp.maximum(peak, piece)
        top = jnp.max(peak, axis=1, keepdims=True)
        mass = jnp.zeros((rows, 128), jnp.float32)
        for b in blocks:
            for half in range(2):
                lanes = slice(128 * half, 128 * half + 128)
                piece = jnp.exp(sbuf[b, :, lanes] - top)
                sbuf[b, :, lanes] = piece
                mass = mass + piece
        inverse = 1.0 / jnp.sum(mass, axis=1, keepdims=True)
        out = jnp.zeros((rows, HEAD_DIM), jnp.float32)
        for b in blocks:
            chip = chip_of(b)
            kx, ky = chip // SIDE, lax.rem(chip, SIDE)
            values = kvg[1, lax.rem(kx + SIDE - x, SIDE), ky].reshape(rows, HEAD_DIM)
            weights = sbuf[b] * inverse
            colacc[b] += jnp.sum(weights.reshape(rows // 8, 8, rows), axis=0)
            out = out + jnp.dot(
                weights.astype(jnp.bfloat16), values, preferred_element_type=jnp.float32
            )
        obuf[:, cols] = out.astype(jnp.bfloat16)
        return carry

    lax.fori_loop(0, half_q // HEAD_DIM, head, 0)

    their_rows = pl.ds(pl.multiple_of(other * shard_rows, 128), shard_rows)
    for b in blocks:
        total = jnp.sum(colacc[b], axis=0, keepdims=True)
        for half in range(2):
            colout[b, half] = total[:, 128 * half : 128 * half + 128]
    for b in range(WINDOW):
        for half in range(2):
            send(
                colout.at[b, half], krecv.at[b, c], SEM_MASS + 2 * b + half,
                at_chip(ch + CHIPS - WINDOW + b, half), SEM_MASS + 2 * b + c,
            )
    send(
        colout.at[WINDOW, other], krecv.at[WINDOW, c], SEM_MASS + 2 * WINDOW + other, partner,
        SEM_MASS + 2 * WINDOW + c,
    )
    krecv[WINDOW, c] = colout[WINDOW, c]
    send(obuf.at[their_rows], orecv, SEM_OUT, partner)
    keep = pltpu.make_async_copy(
        obuf.at[own_rows], att_ref.at[:, columns(c, half_q)], local_sem.at[0]
    )
    keep.start()
    recv(orecv, SEM_OUT)
    put = pltpu.make_async_copy(orecv, att_ref.at[:, columns(other, half_q)], local_sem.at[1])
    put.start()

    for b in range(WINDOW):
        for core in range(2):
            recv(krecv.at[b, core], SEM_MASS + 2 * b + core)
    recv(krecv.at[WINDOW, other], SEM_MASS + 2 * WINDOW + other)
    for core in range(2):
        total = krecv[0, core]
        for b in range(1, WINDOW + 1):
            total = total + krecv[b, core]
        mass_ref[core : core + 1, :] = (total / 8.0).astype(jnp.bfloat16)

    keep.wait()
    put.wait()
    for copy in pending:
        copy.wait_send()

    @pl.when(c == 1)
    def _():
        for core in range(2):
            pltpu.make_async_remote_copy(
                src_ref=act_ref.at[shard_rows - 16 : shard_rows], dst_ref=rows_buf.at[0:16],
                send_sem=send_sem.at[SEM_HALO + core], recv_sem=recv_sem.at[SEM_HALO],
                device_id=at_chip(ch + 1, core), device_id_type=MESH,
            ).wait_send()


def per_device(
    activations, conv_taps, gate_in, gate_out, queries, key_vectors, value_vectors, segment_ids
):
    rows, features = activations.shape
    depth = features // 2
    wt = gate_in.T.reshape(2, 16, 2, depth).transpose(0, 2, 1, 3)
    units = gate_out.reshape(SIDE, SIDE, 2, 2, 16, 8)
    by_y = units[:, :, :, 0].transpose(2, 1, 4, 0, 3).reshape(2, SIDE, 8, 64)
    by_x = units[:, :, :, 1].transpose(2, 0, 4, 1, 3).reshape(2, SIDE, 8, 64)
    none = jnp.zeros_like(by_y)
    gout = jnp.stack(
        [jnp.concatenate([by_y, none], 3), jnp.concatenate([none, by_x], 3)], axis=1
    )
    seg = segment_ids.reshape(-1, 128)
    width = queries.shape[1] // 2
    vmem = pl.BlockSpec(memory_space=pltpu.VMEM)
    anywhere = pl.BlockSpec(memory_space=pl.ANY)
    both = 2 * rows
    bf16, f32 = jnp.bfloat16, jnp.float32
    return pl.pallas_call(
        kernel,
        name="retention_step",
        out_shape=(
            jax.ShapeDtypeStruct((rows, 2 * width), bf16),
            jax.ShapeDtypeStruct((2, rows), bf16),
        ),
        in_specs=[anywhere, vmem, anywhere, vmem, anywhere, anywhere, anywhere, vmem],
        out_specs=(anywhere, vmem),
        scratch_shapes=[
            pltpu.VMEM((both + 16, features), bf16),
            pltpu.VMEM((both, features), bf16),
            pltpu.VMEM((2, SIDE, 2, SIDE, 16, depth), bf16),
            pltpu.VMEM((SIDE, both, 128), f32),
            pltpu.VMEM((SIDE, 3, 64, 128), f32),
            pltpu.VMEM((8, 8, 128), f32),
            pltpu.VMEM((2, 8, 128), f32),
            pltpu.VMEM((CHIPS, 2, 128), f32),
            pltpu.VMEM((2, SIDE, SIDE, 2, rows, HEAD_DIM), bf16),
            pltpu.VMEM((both, width), bf16),
            pltpu.VMEM((both, width), bf16),
            pltpu.VMEM((rows, width), bf16),
            pltpu.VMEM((WINDOW + 1, both, both), f32),
            pltpu.VMEM((both, both), f32),
            pltpu.VMEM((WINDOW + 1, 8, both), f32),
            pltpu.VMEM((WINDOW + 1, 2, 1, 128), f32),
            pltpu.VMEM((WINDOW + 1, 2, 1, 128), f32),
            pltpu.SemaphoreType.DMA((SEMS,)),
            pltpu.SemaphoreType.DMA((SEMS,)),
            pltpu.SemaphoreType.DMA((6,)),
        ],
        compiler_params=pltpu.CompilerParams(collective_id=0, has_side_effects=True),
    )(activations, conv_taps, wt, gout, queries, key_vectors, value_vectors, seg)


def solution(mesh):
    return jax.shard_map(
        per_device,
        mesh=mesh,
        in_specs=(
            P(("dp", "seq"), "heads"),
            P(None, "heads"),
            P("heads", "seq"),
            P(),
            P(("dp", "seq"), "heads"),
            P(("dp", "seq"), "heads"),
            P(("dp", "seq"), "heads"),
            P("dp"),
        ),
        out_specs=(P(("dp", "seq"), "heads"), P("heads", ("dp", "seq"))),
        check_vma=False,
    )
```

time: 627 us -> 66.7 us (0.11); the launches traced: 620 us -> 66.4 us
  waiting for transfers between devices: 311 us -> 0 us
  starting transfers between devices: 104 us -> 0 us
  local copies, waits for them, and re-layouts: 78.5 us -> 4.78 us
  Pallas kernels: 0 us -> 60.3 us
  matrix products: 46 us -> 0 us
  other arithmetic: 28.3 us -> 0.63 us
  blocking collectives: 20.8 us -> 0 us
  loops' own time: 17.7 us -> 0 us
  between operations: 14.3 us -> 0.7 us
    all_gather x3 -> x0, waiting for transfers between devices: 111 us -> none  [the longest x1 59.5 us: per_device(): lax.all_gather(gate_in, 'seq', axis=1, tiled=True)]
    unnamed x6 -> x0, waiting for transfers between devices: 107 us -> none
    ppermute x31 -> x0, starting transfers between devices: 104 us -> none  [the longest x30 98.9 us: partner(): lax.ppermute(x, axis, [(i, i ^ 1 << distance) for i in range(lax.axis_siz...]
    ppermute x31 -> x0, waiting for transfers between devices: 92.5 us -> none  [the longest x30 89.2 us: partner(): lax.ppermute(x, axis, [(i, i ^ 1 << distance) for i in range(lax.axis_siz...]
    pallas_call x0 -> x1, Pallas kernels: none -> 60.3 us  [per_device(): pl.pallas_call(kernel, name='retention_step', out_shape=(jax.ShapeDtypeSt...]
    gather x17 -> x0, local copies, waits for them, and re-layouts: 51.4 us -> none  [the longest x16 50.3 us: visibility(): key_segments = jnp.take(segment_ids, places)]
    dot_general x23 -> x0, matrix products: 46 us -> none  [the longest x14 28 us: block_scores(): jnp.einsum('tgeh,kgh->getk', query_heads, key_block, preferred_element_ty...]
    all_gather x1 -> x0, blocking collectives: 20.8 us -> none  [per_device(): lax.all_gather(own_bias, 'seq', axis=0, tiled=True)]
  transfers between devices with their start and end apart: 36 -> 0, of which waited for: 28 -> 0; matrix products, arithmetic and copies ran while one was open for 4% -> 0% of each run, Pallas kernels for 0% -> 0%
where the time goes in v1:
time: 66.7 us; the launch traced here: 66.4 us
  Pallas kernels  60.3 us (90%)
  local copies, waits for them, and re-layouts  4.78 us (7%)
  between operations  0.7 us (1%)
    pallas_call x1, Pallas kernels, per_device(): pl.pallas_call(kernel, name='retention_step', out_shape=(jax.ShapeDtypeSt...  60.3 us
    unnamed x8, local copies, waits for them, and re-layouts  2.5 us
    reshape x2, local copies, waits for them, and re-layouts, per_device(): wt = gate_in.T.reshape(2, 16, 2, depth).transpose(0, 2, 1, 3)  1.66 us

profile of v1, /device:TPU:1, one launch (start us, length us, event | category | flops | bytes accessed | tf_op | source)
XLA Modules:
  0.0 66.4 jit_solution(7435974076981304143)
XLA Ops:
  0.6 1.0 %reshape.19 = bf16[2,16,2,1024]{3,2,1,0:T(2,128)(2,1)S(1)} reshape(bf16[32,2048]{1,0:T(8,128)(2,1)} %bitcast.24) | data formatting | bytes 262144 | tf_op jit(solution)/shard_map/reshape | solution.py:406
  1.6 0.0 copy-start
  1.6 0.7 %copy.20 = bf16[2,16,2,1024]{3,1,2,0:T(8,128)(2,1)} copy(bf16[2,16,2,1024]{3,2,1,0:T(2,128)(2,1)S(1)} %reshape.19) | data formatting | bytes 262144 | tf_op jit(solution)/shard_map/reshape | solution.py:406
  2.3 0.0 copy-done
  2.3 0.1 reshape.20
  2.5 0.2 fusion
  2.7 0.1 reshape.21
  2.9 0.1 reshape.22
  3.0 0.1 pad_bitcast_fusion
  3.1 0.6 pad_maximum_fusion.gout_ref
  3.7 60.3 %retention_step.1 = (bf16[128,2048]{1,0:T(8,128)(2,1)}, bf16[2,128]{1,0:T(2,128)(2,1)}) custom-call(bf16[128,2048]{1,0:T(8,128)(2,1)} %act_ref.1, bf16[4,2048]{1,0:T(4,128)(2,1)} %taps_ref.1, bf16[2,2,16,1024]{3,2,1,0:T(8,128)(2,1)} %bitcast.21, bf16[2,2,4,8,128]{4,3,2,1,0:T(8,128)(2,1)} %pad_maximum_fusion.gout_ref, bf16[128,2048]{1,0:T(8,128)(2,1)} %q_ref.1, ...), custom_call_target="tpu_custom_call" | custom-call | tf_op jit(solution)/shard_map/retention_step/pallas_call | solution.py:420
  64.0 0.0 copy-start.1
  64.0 1.9 %copy.25 = bf16[128,2048]{1,0:T(8,128)(2,1)} copy(bf16[128,2048]{1,0:T(8,128)(2,1)} %get-tuple-element.8) | data formatting | bytes 1048576
  65.9 0.0 copy-done.1
  65.9 0.5 copy.26
  (2 shorter events, 0.1 us)
Async XLA Ops:
  1.6 0.7 %copy-start = (bf16[1024,8]{0,1:T(8,128)(2,1)S(1)}, bf16[1024,8]{0,1:T(8,128)(2,1)}, u32[]{:S(2)}) copy-start(bf16[1024,8]{0,1:T(8,128)(2,1)} %param.11) | copy-start | bytes 49156
  64.0 1.9 %copy-start.1 = (bf16[2,128]{1,0:T(2,128)(2,1)S(1)}, bf16[2,128]{1,0:T(2,128)(2,1)}, u32[]{:S(2)}) copy-start(bf16[2,128]{1,0:T(2,128)(2,1)} %get-tuple-element.9) | copy-start | bytes 1540

commit v2 on v1

--- a/solution.py
+++ b/solution.py
@@ -10,6 +10,7 @@
 MESH = pl.DeviceIdType.MESH
 HEAD_DIM = 128
 NEG = -1e30
+LOG2E = math.log2(math.e)
 SIDE = 4
 CHIPS = SIDE * SIDE
 WINDOW = 8
@@ -23,14 +24,14 @@
 SEM_RET = SEM_LOGIT + 8
 SEM_MASS = SEM_RET + 16
 SEM_OUT = SEM_MASS + 18
-SEMS = SEM_OUT + 1
+SEMS = SEM_OUT + 8
 
 
 def kernel(
     act_ref, taps_ref, wt_ref, gout_ref, q_ref, k_ref, v_ref, seg_ref,
     att_ref, mass_ref,
-    rows_buf, mixed, wg, part, zrecv, lrecv, rown, rall, kvg, qbuf, obuf, orecv, sbuf, rel,
-    colacc, colout, krecv, send_sem, recv_sem, local_sem,
+    rows_buf, mixed, wg, part, gsel, zrecv, lrecv, rown, rall, kvg, qbuf, obuf, orecv, sbuf, tbuf, tops, rel,
+    colacc, colout, krecv, added, send_sem, recv_sem, local_sem,
 ):
     seq = lax.axis_index("seq")
     h = lax.axis_index("heads")
@@ -41,6 +42,7 @@
     other = 1 - c
     shard_rows = act_ref.shape[0]
     half_q = q_ref.shape[1] // 2
+    depth = act_ref.shape[1] // 2
 
     def at_chip(chip, core):
         return {"seq": lax.rem(chip, CHIPS) * 2 + core}
@@ -65,6 +67,59 @@
                 barrier, inc=1, device_id={"seq": ch * 2 + core, "heads": lax.rem(h + j, 4)},
                 device_id_type=MESH,
             )
+    def columns(which, width):
+        return pl.ds(pl.multiple_of(which * width, width), width)
+
+    own_rows = pl.ds(pl.multiple_of(c * shard_rows, 128), shard_rows)
+    own_rows_in = pl.ds(pl.multiple_of(c * shard_rows + 16, 16), shard_rows)
+
+    def place(t, i):
+        own = x if t == 0 else y
+        return lax.rem(own + (0, 3, 1, 2)[i], SIDE)
+
+    def wslot(t, d, i, ab=None):
+        p = place(t, i)
+        if ab is None:
+            return wg.at[d, t, p]
+        return wg.at[d, t, p, :, ab * depth : (ab + 1) * depth]
+
+    def kvslot(t, d, i, ab=None):
+        p = place(t, i)
+        return kvg.at[t, d, p] if ab is None else kvg.at[t, d, p, ab]
+
+    local = [
+        pltpu.make_async_copy(act_ref, rows_buf.at[own_rows_in], local_sem.at[0]),
+        pltpu.make_async_copy(wt_ref.at[0:16], wslot(0, 0, 0), local_sem.at[1]),
+        pltpu.make_async_copy(wt_ref.at[16:32], wslot(1, 0, 0), local_sem.at[2]),
+        pltpu.make_async_copy(k_ref.at[:, columns(c, 128)], kvg.at[0, 0, x, c], local_sem.at[3]),
+        pltpu.make_async_copy(v_ref.at[:, columns(c, 128)], kvg.at[1, 0, y, c], local_sem.at[4]),
+        pltpu.make_async_copy(q_ref.at[:, columns(c, half_q)], qbuf.at[own_rows], local_sem.at[5]),
+    ]
+    for copy in local:
+        copy.start()
+
+    rows = 2 * shard_rows
+    pos = (ch * rows + lax.broadcasted_iota(jnp.int32, (rows, rows), 0)).astype(jnp.float32)
+    first = jnp.zeros((rows, rows), jnp.float32)
+    seg = seg_ref[...]
+    for number in range(1, 4):
+        count = jnp.sum((seg < number).astype(jnp.float32), axis=1, keepdims=True)
+        count = jnp.sum(count, axis=0, keepdims=True)
+        first = jnp.where(pos >= count, jnp.maximum(first, count), first)
+    rel[...] = first - lax.broadcasted_iota(jnp.int32, (rows, rows), 1).astype(jnp.float32)
+    colacc[...] = jnp.zeros_like(colacc)
+
+    lane = lax.broadcasted_iota(jnp.int32, (1, 128), 1)
+    kind, which, unit = lane // 64, lax.rem(lane // 16, SIDE), lax.rem(lane, 16)
+    for d in range(SIDE):
+        place_x = jnp.where(kind == 0, which, lax.rem(x + d, SIDE))
+        place_y = jnp.where(kind == 0, lax.rem(y + d, SIDE), which)
+        column = ((place_x * SIDE + place_y) * 2 + c) * 32 + kind * 16 + unit
+        pick = lax.broadcasted_iota(jnp.int32, (gout_ref.shape[1], 128), 0) == column
+        pick = jnp.where(pick, 1.0, 0.0).astype(jnp.bfloat16)
+        chosen = jnp.dot(gout_ref[...], pick, preferred_element_type=jnp.float32)
+        gsel[d] = chosen.astype(jnp.bfloat16)
+
     pl.semaphore_wait(barrier, 2 * CHIPS - 1 + 6)
 
     pending = []
@@ -89,18 +144,6 @@
 
     def axis_two(t, step):
         return at_xy(x, y + step) if t == 0 else at_xy(x + step, y)
-
-    def place(t, i):
-        own = x if t == 0 else y
-        return lax.rem(own + (0, 3, 1, 2)[i], SIDE)
-
-    def wslot(t, d, i, ab=None):
-        p = place(t, i)
-        return wg.at[:, d, t, p] if ab is None else wg.at[ab, d, t, p]
-
-    def kvslot(t, d, i, ab=None):
-        p = place(t, i)
-        return kvg.at[t, d, p] if ab is None else kvg.at[t, d, p, ab]
 
     def second_sends(slot, base, t, i, src=None):
         source = slot(t, 0, i) if src is None else src
@@ -149,13 +192,11 @@
                 recv(slot(t, 2, i, 1), sem + 3)
 
     W_BASE, KV_BASE = 0, 2 * GATHER
-    gather_start(wslot, W_BASE, lambda t: wt_ref.at[t])
-
-    own_rows = pl.ds(pl.multiple_of(c * shard_rows, 128), shard_rows)
-    own_rows_in = pl.ds(pl.multiple_of(c * shard_rows + 16, 16), shard_rows)
+    gather_start(wslot, W_BASE, lambda t: wt_ref.at[16 * t : 16 * t + 16])
+
     send(act_ref, rows_buf.at[own_rows_in], SEM_SWAP, partner)
 
-    @pl.when(c == 1)
+    @pl.when((c == 1) & (ch < CHIPS - 1))
     def _():
         for core in range(2):
             pltpu.make_async_remote_copy(
@@ -164,26 +205,15 @@
                 device_id=at_chip(ch + 1, core), device_id_type=MESH,
             ).start()
 
-    def columns(which, width):
-        return pl.ds(pl.multiple_of(which * width, width), width)
-
     send(k_ref.at[:, columns(other, 128)], kvg.at[0, 0, x, c], SEM_SWAP + 2, partner)
     send(v_ref.at[:, columns(other, 128)], kvg.at[1, 0, y, c], SEM_SWAP + 3, partner)
     send(q_ref.at[:, columns(other, half_q)], qbuf.at[own_rows], SEM_SWAP + 1, partner)
-    local = [
-        pltpu.make_async_copy(act_ref, rows_buf.at[own_rows_in], local_sem.at[0]),
-        pltpu.make_async_copy(wt_ref.at[0], wslot(0, 0, 0), local_sem.at[1]),
-        pltpu.make_async_copy(wt_ref.at[1], wslot(1, 0, 0), local_sem.at[2]),
-        pltpu.make_async_copy(k_ref.at[:, columns(c, 128)], kvg.at[0, 0, x, c], local_sem.at[3]),
-        pltpu.make_async_copy(v_ref.at[:, columns(c, 128)], kvg.at[1, 0, y, c], local_sem.at[4]),
-        pltpu.make_async_copy(q_ref.at[:, columns(c, half_q)], qbuf.at[own_rows], local_sem.at[5]),
-    ]
-    for copy in local:
-        copy.start()
-
     gather_first(wslot, W_BASE)
 
-    recv(rows_buf.at[0:16], SEM_HALO)
+    @pl.when(ch > 0)
+    def _():
+        recv(rows_buf.at[0:16], SEM_HALO)
+
     recv(rows_buf.at[pl.ds(pl.multiple_of(other * shard_rows + 16, 16), shard_rows)], SEM_SWAP)
     for copy in local:
         copy.wait()
@@ -209,14 +239,9 @@
     lax.fori_loop(0, (2 * shard_rows // 64) * (mixed.shape[1] // width), mix, 0)
 
     def gate_group(d):
-        depth = mixed.shape[1] // 2
-        total = None
-        for ab in range(2):
-            term = lax.dot_general(
-                mixed[:, ab * depth : (ab + 1) * depth],
-                wg[ab, d].reshape(128, depth), NT, preferred_element_type=jnp.float32,
-            )
-            total = term if total is None else total + term
+        total = lax.dot_general(
+            mixed[...], wg[d].reshape(128, mixed.shape[1]), NT, preferred_element_type=jnp.float32
+        )
         part[d] = total
         for j in range(1, 4):
             peer = lax.rem(h + j, 4)
@@ -244,10 +269,10 @@
         for j in range(3):
             recv(zrecv.at[d, j], SEM_Z + 3 * d + j)
         pre = part[d, pl.ds(pl.multiple_of(h * 64, 64), 64), :]
-        pre = pre + zrecv[d, 0] + zrecv[d, 1] + zrecv[d, 2]
+        for j in range(3):
+            pre = pre + zrecv[d, j]
         hidden = (pre / (1.0 + jnp.exp(-pre))).astype(jnp.bfloat16)
-        gout = gout_ref[c, 0, lax.rem(y + d, SIDE)] + gout_ref[c, 1, lax.rem(x + d, SIDE)]
-        logits = logits + lax.dot_general(gout, hidden, NT, preferred_element_type=jnp.float32)
+        logits = logits + lax.dot_general(gsel[d], hidden, NT, preferred_element_type=jnp.float32)
     mine = 2 * h + c
     lrecv[mine] = jnp.concatenate([logits, jnp.zeros((8, 64), jnp.float32)], 1)
     for j in range(4):
@@ -281,74 +306,106 @@
     gather_last(kvslot, KV_BASE)
     recv(qbuf.at[pl.ds(pl.multiple_of(other * shard_rows, 128), shard_rows)], SEM_SWAP + 1)
 
-    rows = 2 * shard_rows
-    pos = (ch * rows + lax.broadcasted_iota(jnp.int32, (rows, rows), 0)).astype(jnp.float32)
-    first = jnp.zeros((rows, rows), jnp.float32)
-    seg = seg_ref[...]
-    for number in range(1, 4):
-        count = jnp.sum((seg < number).astype(jnp.float32), axis=1, keepdims=True)
-        count = jnp.sum(count, axis=0, keepdims=True)
-        first = jnp.where(pos >= count, jnp.maximum(first, count), first)
-    rel[...] = first - lax.broadcasted_iota(jnp.int32, (rows, rows), 1).astype(jnp.float32)
-    colacc[...] = jnp.zeros_like(colacc)
+    for copy in pending:
+        copy.wait_send()
+    pending.clear()
 
     for i in range(1, CHIPS):
         recv(rall.at[lax.rem(ch + CHIPS - i, CHIPS)], SEM_RET + i)
 
-    scale = 1.0 / math.sqrt(HEAD_DIM)
+    scale = LOG2E / math.sqrt(HEAD_DIM)
     blocks = range(WINDOW + 1)
 
     def chip_of(b):
         return lax.rem(ch + CHIPS - WINDOW + b, CHIPS)
 
-    def head(e, carry):
-        cols = pl.ds(pl.multiple_of(e * HEAD_DIM, HEAD_DIM), HEAD_DIM)
-        query = qbuf[:, cols]
-        peak = jnp.full((rows, 128), NEG, jnp.float32)
+    for b in blocks:
+        bias = rall[chip_of(b)] * LOG2E
+        start = ((ch - WINDOW + b) * rows).astype(jnp.float32)
+        for half in range(2):
+            lanes = slice(128 * half, 128 * half + 128)
+            seen = rel[:, lanes] <= start
+            if b == WINDOW:
+                seen = seen & (
+                    lax.broadcasted_iota(jnp.int32, (rows, 128), 1) + 128 * half
+                    <= lax.broadcasted_iota(jnp.int32, (rows, 128), 0)
+                )
+            added[b, :, lanes] = jnp.where(seen, bias[half : half + 1], NEG)
+
+    their_rows = pl.ds(pl.multiple_of(other * shard_rows, 128), shard_rows)
+
+    def give(e):
+        return pltpu.make_async_remote_copy(
+            src_ref=obuf.at[e, their_rows], dst_ref=orecv.at[e],
+            send_sem=send_sem.at[SEM_OUT + e], recv_sem=recv_sem.at[SEM_OUT + e],
+            device_id=partner, device_id_type=MESH,
+        )
+
+    def key_block(kind, b):
+        chip = chip_of(b)
+        kx, ky = chip // SIDE, lax.rem(chip, SIDE)
+        if kind == 0:
+            block = kvg[0, lax.rem(ky + SIDE - y, SIDE), kx]
+        else:
+            block = kvg[1, lax.rem(kx + SIDE - x, SIDE), ky]
+        return block.reshape(rows, HEAD_DIM)
+
+    def query_of(e):
+        return qbuf[:, pl.ds(pl.multiple_of(e * HEAD_DIM, HEAD_DIM), HEAD_DIM)]
+
+    def score(query, slot, b, peak):
+        scores = lax.dot_general(query, key_block(0, b), NT, preferred_element_type=jnp.float32)
+        scores = scores * scale + added[b]
+        slot[b] = scores
+        return jnp.maximum(peak, jnp.maximum(scores[:, :128], scores[:, 128:]))
+
+    def soften(slot, b, top, mass):
+        piece = jnp.exp2(slot[b] - top)
+        slot[b] = piece
+        return mass + (piece[:, :128] + piece[:, 128:])
+
+    def spread(slot, b, inverse, out):
+        weights = slot[b] * inverse
+        colacc[b] += jnp.sum(weights.reshape(rows // 8, 8, rows), axis=0)
+        return out + jnp.dot(
+            weights.astype(jnp.bfloat16), key_block(1, b), preferred_element_type=jnp.float32
+        )
+
+    low = jnp.full((rows, 128), NEG, jnp.float32)
+    none = jnp.zeros((rows, 128), jnp.float32)
+
+    def finish(e, slot, inverse):
+        out = none
         for b in blocks:
-            chip = chip_of(b)
-            kx, ky = chip // SIDE, lax.rem(chip, SIDE)
-            keys = kvg[0, lax.rem(ky + SIDE - y, SIDE), kx].reshape(rows, HEAD_DIM)
-            bias = rall[chip]
-            scores = lax.dot_general(query, keys, NT, preferred_element_type=jnp.float32) * scale
-            start = ((ch - WINDOW + b) * rows).astype(jnp.float32)
-            for half in range(2):
-                lanes = slice(128 * half, 128 * half + 128)
-                piece = scores[:, lanes] + bias[half : half + 1]
-                seen = rel[:, lanes] <= start
-                if b == WINDOW:
-                    seen = seen & (
-                        lax.broadcasted_iota(jnp.int32, (rows, 128), 1) + 128 * half
-                        <= lax.broadcasted_iota(jnp.int32, (rows, 128), 0)
-                    )
-                piece = jnp.where(seen, piece, NEG)
-                sbuf[b, :, lanes] = piece
-                peak = jnp.maximum(peak, piece)
-        top = jnp.max(peak, axis=1, keepdims=True)
-        mass = jnp.zeros((rows, 128), jnp.float32)
-        for b in blocks:
-            for half in range(2):
-                lanes = slice(128 * half, 128 * half + 128)
-                piece = jnp.exp(sbuf[b, :, lanes] - top)
-                sbuf[b, :, lanes] = piece
-                mass = mass + piece
-        inverse = 1.0 / jnp.sum(mass, axis=1, keepdims=True)
-        out = jnp.zeros((rows, HEAD_DIM), jnp.float32)
-        for b in blocks:
-            chip = chip_of(b)
-            kx, ky = chip // SIDE, lax.rem(chip, SIDE)
-            values = kvg[1, lax.rem(kx + SIDE - x, SIDE), ky].reshape(rows, HEAD_DIM)
-            weights = sbuf[b] * inverse
-            colacc[b] += jnp.sum(weights.reshape(rows // 8, 8, rows), axis=0)
-            out = out + jnp.dot(
-                weights.astype(jnp.bfloat16), values, preferred_element_type=jnp.float32
-            )
-        obuf[:, cols] = out.astype(jnp.bfloat16)
+            out = spread(slot, b, inverse, out)
+        obuf[e] = out.astype(jnp.bfloat16)
+        give(e).start()
+
+    def widest(peak):
+        tops[...] = jnp.broadcast_to(jnp.max(peak, axis=1, keepdims=True), (rows, 128))
+
+    peak = low
+    query = query_of(0)
+    for b in blocks:
+        peak = score(query, sbuf, b, peak)
+    widest(peak)
+    head_count = half_q // HEAD_DIM
+
+    def head_pair(pair, carry):
+        for i, slot, following in ((0, sbuf, tbuf), (1, tbuf, sbuf)):
+            e = 2 * pair + i
+            top = tops[:, :1]
+            query = query_of(jnp.minimum(e + 1, head_count - 1))
+            peak, mass = low, none
+            for b in blocks:
+                peak = score(query, following, b, peak)
+                mass = soften(slot, b, top, mass)
+            finish(e, slot, 1.0 / jnp.sum(mass, axis=1, keepdims=True))
+            widest(peak)
         return carry
 
-    lax.fori_loop(0, half_q // HEAD_DIM, head, 0)
-
-    their_rows = pl.ds(pl.multiple_of(other * shard_rows, 128), shard_rows)
+    lax.fori_loop(0, head_count // 2, head_pair, 0)
+
     for b in blocks:
         total = jnp.sum(colacc[b], axis=0, keepdims=True)
         for half in range(2):
@@ -364,14 +421,19 @@
         SEM_MASS + 2 * WINDOW + c,
     )
     krecv[WINDOW, c] = colout[WINDOW, c]
-    send(obuf.at[their_rows], orecv, SEM_OUT, partner)
-    keep = pltpu.make_async_copy(
-        obuf.at[own_rows], att_ref.at[:, columns(c, half_q)], local_sem.at[0]
-    )
-    keep.start()
-    recv(orecv, SEM_OUT)
-    put = pltpu.make_async_copy(orecv, att_ref.at[:, columns(other, half_q)], local_sem.at[1])
-    put.start()
+    heads = range(half_q // HEAD_DIM)
+    puts = []
+
+    def put(source, e, sem):
+        copy = pltpu.make_async_copy(source, att_ref.at[:, columns(e, HEAD_DIM)], local_sem.at[sem])
+        copy.start()
+        puts.append(copy)
+
+    for e in heads:
+        put(obuf.at[e, own_rows], 8 * c + e, e)
+    for e in heads:
+        give(e).wait()
+        put(orecv.at[e], 8 * other + e, 8 + e)
 
     for b in range(WINDOW):
         for core in range(2):
@@ -383,12 +445,12 @@
             total = total + krecv[b, core]
         mass_ref[core : core + 1, :] = (total / 8.0).astype(jnp.bfloat16)
 
-    keep.wait()
-    put.wait()
+    for copy in puts:
+        copy.wait()
     for copy in pending:
         copy.wait_send()
 
-    @pl.when(c == 1)
+    @pl.when((c == 1) & (ch < CHIPS - 1))
     def _():
         for core in range(2):
             pltpu.make_async_remote_copy(
@@ -402,15 +464,6 @@
     activations, conv_taps, gate_in, gate_out, queries, key_vectors, value_vectors, segment_ids
 ):
     rows, features = activations.shape
-    depth = features // 2
-    wt = gate_in.T.reshape(2, 16, 2, depth).transpose(0, 2, 1, 3)
-    units = gate_out.reshape(SIDE, SIDE, 2, 2, 16, 8)
-    by_y = units[:, :, :, 0].transpose(2, 1, 4, 0, 3).reshape(2, SIDE, 8, 64)
-    by_x = units[:, :, :, 1].transpose(2, 0, 4, 1, 3).reshape(2, SIDE, 8, 64)
-    none = jnp.zeros_like(by_y)
-    gout = jnp.stack(
-        [jnp.concatenate([by_y, none], 3), jnp.concatenate([none, by_x], 3)], axis=1
-    )
     seg = segment_ids.reshape(-1, 128)
     width = queries.shape[1] // 2
     vmem = pl.BlockSpec(memory_space=pltpu.VMEM)
@@ -429,27 +482,31 @@
         scratch_shapes=[
             pltpu.VMEM((both + 16, features), bf16),
             pltpu.VMEM((both, features), bf16),
-            pltpu.VMEM((2, SIDE, 2, SIDE, 16, depth), bf16),
+            pltpu.VMEM((SIDE, 2, SIDE, 16, features), bf16),
             pltpu.VMEM((SIDE, both, 128), f32),
+            pltpu.VMEM((SIDE, 8, 128), bf16),
             pltpu.VMEM((SIDE, 3, 64, 128), f32),
             pltpu.VMEM((8, 8, 128), f32),
             pltpu.VMEM((2, 8, 128), f32),
             pltpu.VMEM((CHIPS, 2, 128), f32),
             pltpu.VMEM((2, SIDE, SIDE, 2, rows, HEAD_DIM), bf16),
             pltpu.VMEM((both, width), bf16),
-            pltpu.VMEM((both, width), bf16),
-            pltpu.VMEM((rows, width), bf16),
+            pltpu.VMEM((8, both, HEAD_DIM), bf16),
+            pltpu.VMEM((8, rows, HEAD_DIM), bf16),
             pltpu.VMEM((WINDOW + 1, both, both), f32),
+            pltpu.VMEM((WINDOW + 1, both, both), f32),
+            pltpu.VMEM((both, 128), f32),
             pltpu.VMEM((both, both), f32),
             pltpu.VMEM((WINDOW + 1, 8, both), f32),
             pltpu.VMEM((WINDOW + 1, 2, 1, 128), f32),
             pltpu.VMEM((WINDOW + 1, 2, 1, 128), f32),
+            pltpu.VMEM((WINDOW + 1, both, both), f32),
             pltpu.SemaphoreType.DMA((SEMS,)),
             pltpu.SemaphoreType.DMA((SEMS,)),
-            pltpu.SemaphoreType.DMA((6,)),
+            pltpu.SemaphoreType.DMA((16,)),
         ],
         compiler_params=pltpu.CompilerParams(collective_id=0, has_side_effects=True),
-    )(activations, conv_taps, wt, gout, queries, key_vectors, value_vectors, seg)
+    )(activations, conv_taps, gate_in.T, gate_out.T, queries, key_vectors, value_vectors, seg)
 
 
 def solution(mesh):

time: 66.7 us -> 61.5 us (0.922)
  local copies, waits for them, and re-layouts: 4.78 us -> 2.4 us
  Pallas kernels: 60.3 us -> 58.2 us
    pallas_call x1, Pallas kernels: 60.3 us -> 58.2 us  [per_device(): pl.pallas_call(kernel, name='retention_step', out_shape=(jax.ShapeDtypeSt...]
    reshape x5 -> x0, local copies, waits for them, and re-layouts: 2.01 us -> none  [the longest x2 1.66 us: per_device(): wt = gate_in.T.reshape(2, 16, 2, depth).transpose(0, 2, 1, 3)]
    unnamed x8 -> x4, local copies, waits for them, and re-layouts: 2.5 us -> 2.4 us
where the time goes in v2:
time: 61.5 us; the launch traced here: 61.3 us
  Pallas kernels  58.2 us (95%)
  local copies, waits for them, and re-layouts  2.4 us (4%)
  between operations  0.65 us (1%)
    pallas_call x1, Pallas kernels, per_device(): pl.pallas_call(kernel, name='retention_step', out_shape=(jax.ShapeDtypeSt...  58.2 us
    unnamed x4, local copies, waits for them, and re-layouts  2.4 us

profile of v2, /device:TPU:1, one launch (start us, length us, event | category | flops | bytes accessed | tf_op | source)
XLA Modules:
  0.0 61.3 jit_solution(1976382560426182393)
XLA Ops:
  0.6 58.2 %retention_step.1 = (bf16[128,2048]{1,0:T(8,128)(2,1)}, bf16[2,128]{1,0:T(2,128)(2,1)}) custom-call(bf16[128,2048]{1,0:T(8,128)(2,1)} %act_ref.1, bf16[4,2048]{1,0:T(4,128)(2,1)} %taps_ref.1, bf16[32,2048]{1,0:T(8,128)(2,1)} %bitcast.3, bf16[8,1024]{1,0:T(8,128)(2,1)} %bitcast.4, bf16[128,2048]{1,0:T(8,128)(2,1)} %q_ref.1, bf16[128,256]{1,0:T(8,128)(2,1)} %k_ref.1, ...), custom_call_target="tpu_custom_call" | custom-call | tf_op jit(solution)/shard_map/retention_step/pallas_call | solution.py:473
  58.9 0.0 copy-start
  58.9 1.9 %copy.12 = bf16[128,2048]{1,0:T(8,128)(2,1)} copy(bf16[128,2048]{1,0:T(8,128)(2,1)} %get-tuple-element.4) | data formatting | bytes 1048576
  60.8 0.0 copy-done
  60.8 0.5 copy.13
Async XLA Ops:
  58.9 1.9 %copy-start = (bf16[2,128]{1,0:T(2,128)(2,1)S(1)}, bf16[2,128]{1,0:T(2,128)(2,1)}, u32[]{:S(2)}) copy-start(bf16[2,128]{1,0:T(2,128)(2,1)} %get-tuple-element.5) | copy-start | bytes 1540

commit v3 on v2

--- a/solution.py
+++ b/solution.py
@@ -159,7 +159,7 @@
         for t in range(2):
             second_sends(slot, base, t, 0, source(t))
 
-    def gather_first(slot, base):
+    def gather_first(slot, base, between=None):
         for t in range(2):
             sem = base + t * GATHER
             recv(slot(t, 0, 1), sem)
@@ -169,6 +169,8 @@
         for i in (1, 2):
             for t in range(2):
                 second_sends(slot, base, t, i)
+        if between is not None:
+            between()
         for t in range(2):
             sem = base + t * GATHER
             recv(slot(t, 0, 3, 0), sem + 2)
@@ -192,10 +194,6 @@
                 recv(slot(t, 2, i, 1), sem + 3)
 
     W_BASE, KV_BASE = 0, 2 * GATHER
-    gather_start(wslot, W_BASE, lambda t: wt_ref.at[16 * t : 16 * t + 16])
-
-    send(act_ref, rows_buf.at[own_rows_in], SEM_SWAP, partner)
-
     @pl.when((c == 1) & (ch < CHIPS - 1))
     def _():
         for core in range(2):
@@ -205,38 +203,43 @@
                 device_id=at_chip(ch + 1, core), device_id_type=MESH,
             ).start()
 
+    gather_start(wslot, W_BASE, lambda t: wt_ref.at[16 * t : 16 * t + 16])
+
+    send(act_ref, rows_buf.at[own_rows_in], SEM_SWAP, partner)
+
     send(k_ref.at[:, columns(other, 128)], kvg.at[0, 0, x, c], SEM_SWAP + 2, partner)
     send(v_ref.at[:, columns(other, 128)], kvg.at[1, 0, y, c], SEM_SWAP + 3, partner)
     send(q_ref.at[:, columns(other, half_q)], qbuf.at[own_rows], SEM_SWAP + 1, partner)
-    gather_first(wslot, W_BASE)
-
-    @pl.when(ch > 0)
-    def _():
-        recv(rows_buf.at[0:16], SEM_HALO)
-
-    recv(rows_buf.at[pl.ds(pl.multiple_of(other * shard_rows + 16, 16), shard_rows)], SEM_SWAP)
-    for copy in local:
-        copy.wait()
-
-    @pl.when(ch == 0)
-    def _():
-        rows_buf[0:16, :] = jnp.zeros((16, rows_buf.shape[1]), jnp.bfloat16)
-
-    width = 512
-    tap_count = taps_ref.shape[0]
-
-    def mix(step, carry):
-        r0 = pl.multiple_of((step // 4) * 64, 64)
-        cols = pl.ds(pl.multiple_of(lax.rem(step, 4) * width, width), width)
-        block = rows_buf[pl.ds(r0, 80), cols].astype(jnp.float32)
-        total = jnp.zeros((64, width), jnp.float32)
-        for tap in range(tap_count):
-            moved = block if tap == 0 else pltpu.roll(block, tap, axis=0)
-            total = total + taps_ref[tap : tap + 1, cols].astype(jnp.float32) * moved[16:80]
-        mixed[pl.ds(r0, 64), cols] = total.astype(jnp.bfloat16)
-        return carry
-
-    lax.fori_loop(0, (2 * shard_rows // 64) * (mixed.shape[1] // width), mix, 0)
+    def convolve():
+        @pl.when(ch > 0)
+        def _():
+            recv(rows_buf.at[0:16], SEM_HALO)
+
+        recv(rows_buf.at[pl.ds(pl.multiple_of(other * shard_rows + 16, 16), shard_rows)], SEM_SWAP)
+        for copy in local:
+            copy.wait()
+
+        @pl.when(ch == 0)
+        def _():
+            rows_buf[0:16, :] = jnp.zeros((16, rows_buf.shape[1]), jnp.bfloat16)
+
+        width = 512
+        tap_count = taps_ref.shape[0]
+
+        def mix(step, carry):
+            r0 = pl.multiple_of((step // 4) * 64, 64)
+            cols = pl.ds(pl.multiple_of(lax.rem(step, 4) * width, width), width)
+            block = rows_buf[pl.ds(r0, 80), cols].astype(jnp.float32)
+            total = jnp.zeros((64, width), jnp.float32)
+            for tap in range(tap_count):
+                moved = block if tap == 0 else pltpu.roll(block, tap, axis=0)
+                total = total + taps_ref[tap : tap + 1, cols].astype(jnp.float32) * moved[16:80]
+            mixed[pl.ds(r0, 64), cols] = total.astype(jnp.bfloat16)
+            return carry
+
+        lax.fori_loop(0, (2 * shard_rows // 64) * (mixed.shape[1] // width), mix, 0)
+
+    gather_first(wslot, W_BASE, convolve)
 
     def gate_group(d):
         total = lax.dot_general(
@@ -380,6 +383,7 @@
             out = spread(slot, b, inverse, out)
         obuf[e] = out.astype(jnp.bfloat16)
         give(e).start()
+        att_ref[:, columns(8 * c + e, HEAD_DIM)] = obuf[e, own_rows, :]
 
     def widest(peak):
         tops[...] = jnp.broadcast_to(jnp.max(peak, axis=1, keepdims=True), (rows, 128))
@@ -421,19 +425,9 @@
         SEM_MASS + 2 * WINDOW + c,
     )
     krecv[WINDOW, c] = colout[WINDOW, c]
-    heads = range(half_q // HEAD_DIM)
-    puts = []
-
-    def put(source, e, sem):
-        copy = pltpu.make_async_copy(source, att_ref.at[:, columns(e, HEAD_DIM)], local_sem.at[sem])
-        copy.start()
-        puts.append(copy)
-
-    for e in heads:
-        put(obuf.at[e, own_rows], 8 * c + e, e)
-    for e in heads:
+    for e in range(half_q // HEAD_DIM):
         give(e).wait()
-        put(orecv.at[e], 8 * other + e, 8 + e)
+        att_ref[:, columns(8 * other + e, HEAD_DIM)] = orecv[e]
 
     for b in range(WINDOW):
         for core in range(2):
@@ -445,8 +439,6 @@
             total = total + krecv[b, core]
         mass_ref[core : core + 1, :] = (total / 8.0).astype(jnp.bfloat16)
 
-    for copy in puts:
-        copy.wait()
     for copy in pending:
         copy.wait_send()
 
@@ -474,11 +466,11 @@
         kernel,
         name="retention_step",
         out_shape=(
-            jax.ShapeDtypeStruct((rows, 2 * width), bf16),
-            jax.ShapeDtypeStruct((2, rows), bf16),
+            pltpu.VMEM((rows, 2 * width), bf16),
+            pltpu.VMEM((2, rows), bf16),
         ),
         in_specs=[anywhere, vmem, anywhere, vmem, anywhere, anywhere, anywhere, vmem],
-        out_specs=(anywhere, vmem),
+        out_specs=(vmem, vmem),
         scratch_shapes=[
             pltpu.VMEM((both + 16, features), bf16),
             pltpu.VMEM((both, features), bf16),
@@ -503,7 +495,7 @@
             pltpu.VMEM((WINDOW + 1, both, both), f32),
             pltpu.SemaphoreType.DMA((SEMS,)),
             pltpu.SemaphoreType.DMA((SEMS,)),
-            pltpu.SemaphoreType.DMA((16,)),
+            pltpu.SemaphoreType.DMA((6,)),
         ],
         compiler_params=pltpu.CompilerParams(collective_id=0, has_side_effects=True),
     )(activations, conv_taps, gate_in.T, gate_out.T, queries, key_vectors, value_vectors, seg)

time: 61.5 us -> 60.3 us (0.980)
  local copies, waits for them, and re-layouts: 2.4 us -> 1.31 us
    unnamed x4 -> x2, local copies, waits for them, and re-layouts: 2.4 us -> 1.31 us
where the time goes in v3:
time: 60.3 us; the launch traced here: 60 us
  Pallas kernels  58.1 us (96%)
  local copies, waits for them, and re-layouts  1.31 us (2%)
  between operations  0.64 us (1%)
    pallas_call x1, Pallas kernels, per_device(): pl.pallas_call(kernel, name='retention_step', out_shape=(pltpu.VMEM((rows...  58.1 us
    unnamed x2, local copies, waits for them, and re-layouts  1.31 us

profile of v3, /device:TPU:1, one launch (start us, length us, event | category | flops | bytes accessed | tf_op | source)
XLA Modules:
  0.0 60.0 jit_solution(15369808764357263808)
XLA Ops:
  0.6 58.1 %retention_step.1 = (bf16[128,2048]{1,0:T(8,128)(2,1)S(1)}, bf16[2,128]{1,0:T(2,128)(2,1)S(1)}) custom-call(bf16[128,2048]{1,0:T(8,128)(2,1)} %act_ref.1, bf16[4,2048]{1,0:T(4,128)(2,1)} %taps_ref.1, bf16[32,2048]{1,0:T(8,128)(2,1)} %bitcast.3, bf16[8,1024]{1,0:T(8,128)(2,1)} %bitcast.4, bf16[128,2048]{1,0:T(8,128)(2,1)} %q_ref.1, bf16[128,256]{1,0:T(8,128)(2,1)} %k_ref.1, ...), custom_call_target="tpu_custom_call" | custom-call | tf_op jit(solution)/shard_map/retention_step/pallas_call | solution.py:465
  58.7 0.8 %copy.12 = bf16[128,2048]{1,0:T(8,128)(2,1)} copy(bf16[128,2048]{1,0:T(8,128)(2,1)S(1)} %get-tuple-element.2) | data formatting | bytes 1048576
  59.5 0.5 copy.13

commit v4 on v3

--- a/solution.py
+++ b/solution.py
@@ -145,11 +145,22 @@
     def axis_two(t, step):
         return at_xy(x, y + step) if t == 0 else at_xy(x + step, y)
 
+    def unseen(base, t, i):
+        return base == 2 * GATHER and t == 0 and i == 2
+
+    def left_part(base, t):
+        return 1 if base == 2 * GATHER and t == 1 else None
+
     def second_sends(slot, base, t, i, src=None):
+        if unseen(base, t, i):
+            return
         source = slot(t, 0, i) if src is None else src
         sem = base + t * GATHER + 4 + 4 * i
         send(source, slot(t, 3, i), sem, axis_two(t, 1))
-        send(source, slot(t, 1, i), sem + 1, axis_two(t, 3))
+        part_left = left_part(base, t)
+        if part_left is not None:
+            source = slot(t, 0, i, part_left)
+        send(source, slot(t, 1, i, part_left), sem + 1, axis_two(t, 3))
 
     def gather_start(slot, base, source):
         for t in range(2):
@@ -180,15 +191,19 @@
     def gather_second(slot, base):
         for i in range(4):
             for t in range(2):
+                if unseen(base, t, i):
+                    continue
                 sem = base + t * GATHER + 4 + 4 * i
                 recv(slot(t, 3, i), sem)
                 send(slot(t, 3, i, 0), slot(t, 2, i, 0), sem + 2, axis_two(t, 1))
-                recv(slot(t, 1, i), sem + 1)
+                recv(slot(t, 1, i, left_part(base, t)), sem + 1)
                 send(slot(t, 1, i, 1), slot(t, 2, i, 1), sem + 3, axis_two(t, 3))
 
     def gather_last(slot, base):
         for i in range(4):
             for t in range(2):
+                if unseen(base, t, i):
+                    continue
                 sem = base + t * GATHER + 4 + 4 * i
                 recv(slot(t, 2, i, 0), sem + 2)
                 recv(slot(t, 2, i, 1), sem + 3)

time: 60.3 us -> 60.3 us (level)
  no operation moved by 1% of the time
where the time goes in v4:
time: 60.3 us; the launch traced here: 60 us
  Pallas kernels  58.1 us (96%)
  local copies, waits for them, and re-layouts  1.31 us (2%)
  between operations  0.64 us (1%)
    pallas_call x1, Pallas kernels, per_device(): pl.pallas_call(kernel, name='retention_step', out_shape=(pltpu.VMEM((rows...  58.1 us
    unnamed x2, local copies, waits for them, and re-layouts  1.31 us

profile of v4, /device:TPU:1, one launch (start us, length us, event | category | flops | bytes accessed | tf_op | source)
XLA Modules:
  0.0 60.0 jit_solution(16504193846108820597)
XLA Ops:
  0.6 58.1 %retention_step.1 = (bf16[128,2048]{1,0:T(8,128)(2,1)S(1)}, bf16[2,128]{1,0:T(2,128)(2,1)S(1)}) custom-call(bf16[128,2048]{1,0:T(8,128)(2,1)} %act_ref.1, bf16[4,2048]{1,0:T(4,128)(2,1)} %taps_ref.1, bf16[32,2048]{1,0:T(8,128)(2,1)} %bitcast.3, bf16[8,1024]{1,0:T(8,128)(2,1)} %bitcast.4, bf16[128,2048]{1,0:T(8,128)(2,1)} %q_ref.1, bf16[128,256]{1,0:T(8,128)(2,1)} %k_ref.1, ...), custom_call_target="tpu_custom_call" | custom-call | tf_op jit(solution)/shard_map/retention_step/pallas_call | solution.py:480
  58.7 0.8 %copy.12 = bf16[128,2048]{1,0:T(8,128)(2,1)} copy(bf16[128,2048]{1,0:T(8,128)(2,1)S(1)} %get-tuple-element.2) | data formatting | bytes 1048576
  59.5 0.5 copy.13
